TPU v7x, 32 devices: a whole 2x2x4 slice. The times are simulated.
32 devices in a mesh: scene: 2 (over y), tok: 8 (over z, x), hid: 2 (over core).
Axes of the slice: x: 2, y: 2, z: 4, core: 2. Of those that a mesh axis runs over, the one named last changes fastest.
Arguments:
- input_keys: bfloat16 [16384, 384], P(('scene', 'tok'), 'hid'), parts along dimension 0, may hold values from -6 to 6
- input_values: bfloat16 [16384, 384], P(('scene', 'tok'), 'hid'), parts along dimension 0, may hold values from -6 to 6
- input_lr: float32 [16384], P(('scene', 'tok')), parts along dimension 0, may hold values from 0.1 to 1
- gate_weight: bfloat16 [384, 1536], P('tok', 'hid'), may hold values from -0.3125 to 0.3125
- up_weight: bfloat16 [384, 1536], P('tok', 'hid'), may hold values from -0.3125 to 0.3125
- down_weight: bfloat16 [384, 1536], P('tok', 'hid'), may hold values from -0.15625 to 0.15625
- queries: bfloat16 [2048, 384], P(('scene', 'tok'), 'hid'), parts along dimension 0, may hold values from -6 to 6
- out_grad: bfloat16 [2048, 384], P(('scene', 'tok'), 'hid'), parts along dimension 0, may hold values from -6 to 6
Outputs:
- target_out: bfloat16 [2048, 384], P(('scene', 'tok'), 'hid'), parts along dimension 0
- query_grad: bfloat16 [2048, 384], P(('scene', 'tok'), 'hid'), parts along dimension 0
There are 2 independent parts, one for each index of `scene`. A program takes and returns all parts, laid end to end along the dimension named above; an argument that names none is the same for every part. Nothing has to cross between parts.
All inputs are finite; a program needn't handle non-finite values.
Results may differ from a plain program's by a relative error of at most 0.009.
Values may be sent and summed in bfloat16 or wider, within the bound.
A program may use at most 64 MiB of HBM per device.

v0:
```python
import jax
import jax.numpy as jnp
from jax import lax
from jax.sharding import PartitionSpec as P

HID = 1536
step_ratio = 0.5
epsilon = 1e-06


def silu_slope(pre):
    sigma = jax.nn.sigmoid(pre)
    return sigma * (1.0 + pre * (1.0 - sigma))


def contract_rows(left, right):
    return lax.dot_general(
        left, right, (((0,), (0,)), ((), ())), preferred_element_type=jnp.float32
    )


def contract_cols(left, right):
    return lax.dot_general(
        left, right, (((1,), (1,)), ((), ())), preferred_element_type=jnp.float32
    )


def finish(moved, wsq, msq):
    return (moved * (jnp.sqrt(wsq) / jnp.sqrt(msq + epsilon))[:, None]).astype(jnp.bfloat16)


def shards(
    input_keys, input_values, input_lr, gate_weight, up_weight, down_weight, queries, out_grad
):
    keys, values = (
        lax.all_gather(input_keys, "hid", axis=1, tiled=True),
        lax.all_gather(input_values, "hid", axis=1, tiled=True),
    )
    w_gate, w_up, w_down = (
        lax.all_gather(gate_weight, "tok", axis=0, tiled=True),
        lax.all_gather(up_weight, "tok", axis=0, tiled=True),
        lax.all_gather(down_weight, "tok", axis=0, tiled=True),
    )
    scaled = (input_lr[:, None] * values.astype(jnp.float32)).astype(jnp.bfloat16)
    key_gate = jnp.dot(keys, w_gate, preferred_element_type=jnp.float32)
    key_up = jnp.dot(keys, w_up, preferred_element_type=jnp.float32)
    gate_act = jax.nn.silu(key_gate)
    key_act = (gate_act * key_up).astype(jnp.bfloat16)
    back = jnp.dot(scaled, w_down, preferred_element_type=jnp.float32)
    d_gate = (-back * key_up * silu_slope(key_gate)).astype(jnp.bfloat16)
    d_up = (-back * gate_act).astype(jnp.bfloat16)
    width = gate_weight.shape[1]
    grads = lax.psum(
        jnp.concatenate(
            [
                contract_rows(keys, d_gate),
                contract_rows(keys, d_up),
                -contract_rows(scaled, key_act),
            ],
            axis=1,
        ),
        "tok",
    )
    olds = (w_gate, w_up, w_down)
    pieces = [grads[:, :width], grads[:, width : 2 * width], grads[:, 2 * width :]]
    weights = [old.astype(jnp.float32) for old in olds]
    renewed = []
    stats = []
    for weight, grad in zip(weights, pieces):
        stats.append(jnp.sum(weight * weight, axis=1))
        stats.append(jnp.sum(weight * grad, axis=1))
        stats.append(jnp.sum(grad * grad, axis=1))
    totals = lax.psum(
        (stats[0], stats[1], stats[2], stats[3], stats[4], stats[5], stats[6], stats[7], stats[8]),
        "hid",
    )
    for index in range(3):
        wsq = totals[3 * index] / HID
        cross = totals[3 * index + 1] / HID
        gsq = totals[3 * index + 2] / HID
        scale = step_ratio * jnp.sqrt(wsq) / jnp.sqrt(gsq + epsilon)
        moved = weights[index] - scale[:, None] * pieces[index]
        msq = wsq - 2.0 * scale * cross + scale * scale * gsq
        renewed.append(finish(moved, wsq, msq))
    new_gate, new_up, new_down = (renewed[0], renewed[1], renewed[2])
    query_rows, grad_rows = (
        lax.all_gather(queries, "hid", axis=1, tiled=True),
        lax.all_gather(out_grad, "hid", axis=1, tiled=True),
    )
    query_gate = jnp.dot(query_rows, new_gate, preferred_element_type=jnp.float32)
    query_up = jnp.dot(query_rows, new_up, preferred_element_type=jnp.float32)
    query_silu = jax.nn.silu(query_gate)
    query_act = (query_silu * query_up).astype(jnp.bfloat16)
    out_part = contract_cols(query_act, new_down)
    query_back = jnp.dot(grad_rows, new_down, preferred_element_type=jnp.float32)
    q_gate_grad = (query_back * query_up * silu_slope(query_gate)).astype(jnp.bfloat16)
    q_up_grad = (query_back * query_silu).astype(jnp.bfloat16)
    grad_part = contract_cols(q_gate_grad, new_gate) + contract_cols(q_up_grad, new_up)
    out_sum, grad_sum = (
        lax.psum_scatter(
            out_part.astype(jnp.bfloat16), "hid", scatter_dimension=1, tiled=True
        ).astype(jnp.float32),
        lax.psum_scatter(
            grad_part.astype(jnp.bfloat16), "hid", scatter_dimension=1, tiled=True
        ).astype(jnp.float32),
    )
    return (out_sum.astype(jnp.bfloat16), grad_sum.astype(jnp.bfloat16))


def solution(mesh):
    return jax.shard_map(
        shards,
        mesh=mesh,
        in_specs=(
            P(("scene", "tok"), "hid"),
            P(("scene", "tok"), "hid"),
            P(("scene", "tok")),
            P("tok", "hid"),
            P("tok", "hid"),
            P("tok", "hid"),
            P(("scene", "tok"), "hid"),
            P(("scene", "tok"), "hid"),
        ),
        out_specs=(P(("scene", "tok"), "hid"), P(("scene", "tok"), "hid")),
        check_vma=False,
    )
```

profile of v0, /device:TPU:0, one launch (start us, length us, event | category | flops | bytes accessed | tf_op | source)
XLA Modules:
  0.0 297.7 jit_solution(15559393787212214560)
XLA Ops:
  7.2 2.7 all_gather.24
  9.9 33.4 %all_gather.21 = bf16[384,768]{1,0:T(8,128)(2,1)S(1)} all-gather(bf16[48,768]{1,0:T(8,128)(2,1)} %param.11), channel_id=1, replica_groups=mesh['scene'=2,'tok'=8,'hid'=2] {'tok'}, dimensions={0}, use_global_device_ids=true | all-gather | bytes 663552 | tf_op jit(solution)/shard_map/all_gather | solution.py:40
  43.4 31.3 %all_gather.25 = bf16[384,768]{1,0:T(8,128)(2,1)S(1)} all-gather(bf16[48,768]{1,0:T(8,128)(2,1)S(1)} %copy-done.6), channel_id=1, replica_groups=mesh['scene'=2,'tok'=8,'hid'=2] {'tok'}, dimensions={0}, use_global_device_ids=true | all-gather | bytes 663552 | tf_op jit(solution)/shard_map/all_gather | solution.py:41
  74.6 1.0 fusion.34
  75.7 1.0 fusion.33
  76.7 2.4 all_gather.22
  79.1 31.4 %all_gather.23 = bf16[384,768]{1,0:T(8,128)(2,1)S(1)} all-gather(bf16[48,768]{1,0:T(8,128)(2,1)S(1)} %copy-done.7), channel_id=1, replica_groups=mesh['scene'=2,'tok'=8,'hid'=2] {'tok'}, dimensions={0}, use_global_device_ids=true | all-gather | bytes 663552 | tf_op jit(solution)/shard_map/all_gather | solution.py:42
  110.5 1.0 fusion.20
  111.6 1.2 fusion.6
  112.8 1.5 fusion.4
  114.3 1.3 fusion.5
  115.6 2.0 pad_maximum_fusion
  117.7 1.1 copy.14
  118.8 1.1 copy.16
  119.8 1.1 copy.17
  121.0 2.0 all_gather.27
  123.0 2.0 all_gather.26
  125.0 132.9 %all-reduce.3.cloned.1.call-done = f32[384,2304]{0,1:T(8,128)} async-done(((f32[384,2304]{0,1:T(8,128)}), f32[384,2304]{0,1:T(8,128)}) %all-reduce.3.cloned.1.call-update) | async-done | bytes 3538960 | tf_op jit(solution)/shard_map/psum | solution.py:53
  257.9 4.1 %multiply_reduce_fusion.2 = (f32[384]{0:T(512)S(1)}, f32[384]{0:T(512)S(1)}, f32[384]{0:T(512)S(1)}, f32[384]{0:T(512)S(1)}, f32[384]{0:T(512)}, /*index=5*/f32[...) fusion(f32[384,2304]{0,1:T(8,128)} %all-reduce.3.cloned.1.call-done, bf16[384,768]{0,1:T(8,128)(2,1)} %copy.14, ...), kind=kLoop, calls=%fused_computation.39 | loop fusion | flops 6189696 | bytes 5322240 | tf_op jit(solution)/shard_map/reduce_sum | solution.py:72
  261.9 4.6 %all-reduce = (f32[384]{0:T(512)}, f32[384]{0:T(512)}, f32[384]{0:T(512)}, f32[384]{0:T(512)}, f32[384]{0:T(512)}, /*index=5*/f32[384]{0:T(512)}, f32[384]{0:T(512)}, f32[384]{0:T(512)}, f32[384]{0:T(512)}) all-reduce(f32[384]{0:T(512)S(1)} %get-tuple-element.5, ...), channel_id=1, replica_groups=mesh['scene'=2,'tok'=8,'hid'=2] {'hid'}, use_global_device_ids=true, to_apply=%region_18.19 | all-reduce | flops 3456 | bytes 27648 | tf_op jit(solution)/shard_map/psum | solution.py:73
  266.5 0.7 rsqrt_multiply_fusion.5
  267.2 0.8 rsqrt_multiply_fusion.1
  268.0 2.0 fusion.9
  270.1 0.3 convolution_bitcast_fusion.1
  270.4 0.3 convolution_bitcast_fusion.2
  270.7 0.3 copy-done.4
  271.0 0.3 convolution_bitcast_fusion
  271.4 0.5 fusion.24
  271.8 1.1 fusion.19
  273.0 1.0 convolution_convert_fusion
  274.0 5.6 %reduce-scatter.5.cloned.1.call-done = bf16[128,192]{0,1:T(8,128)(2,1)} async-done(((bf16[128,384]{0,1:T(8,128)(2,1)}), bf16[128,192]{0,1:T(8,128)(2,1)}) %reduce-scatter.5.cloned.1.call-update) | async-done | bytes 49168 | tf_op jit(solution)/shard_map/reduce_scatter | solution.py:103
  279.7 11.5 %reduce-scatter.3.cloned.1.call-done = bf16[128,192]{0,1:T(8,128)(2,1)} async-done(((bf16[128,384]{0,1:T(8,128)(2,1)}), bf16[128,192]{0,1:T(8,128)(2,1)}) %reduce-scatter.3.cloned.1.call-update) | async-done | bytes 49168 | tf_op jit(solution)/shard_map/reduce_scatter | solution.py:100
  (27 shorter events, 0.2 us)
Async XLA Ops:
  7.2 36.2 %copy-start.6 = (bf16[48,768]{1,0:T(8,128)(2,1)S(1)}, bf16[48,768]{1,0:T(8,128)(2,1)}, u32[]{:S(2)}) copy-start(bf16[48,768]{1,0:T(8,128)(2,1)} %param.12) | copy-start | bytes 221188
  7.2 250.7 %all-reduce.3.cloned.1.call-start = ((), (), s32[]{:S(2)}) async-start(), calls=%async_computation.2 | async-start | bytes 7077888 | tf_op jit(solution)/shard_map/psum | solution.py:53
  75.7 1.1 copy-start.5
  75.7 3.4 %copy-start.7 = (bf16[48,768]{1,0:T(8,128)(2,1)S(1)}, bf16[48,768]{1,0:T(8,128)(2,1)}, u32[]{:S(2)}) copy-start(bf16[48,768]{1,0:T(8,128)(2,1)} %param.13) | copy-start | bytes 221188
  76.7 33.8 %copy-start.10 = (f32[1024]{0:T(1024)S(1)}, f32[1024]{0:T(1024)}, u32[]{:S(2)}) copy-start(f32[1024]{0:T(1024)} %param.10) | copy-start | bytes 12292
  117.7 3.3 %copy-start.8 = (bf16[128,192]{0,1:T(8,128)(2,1)S(1)}, bf16[128,192]{0,1:T(8,128)(2,1)}, u32[]{:S(2)}) copy-start(bf16[128,192]{0,1:T(8,128)(2,1)} %param.15) | copy-start | bytes 147460
  117.7 5.3 %copy-start.9 = (bf16[128,192]{0,1:T(8,128)(2,1)S(1)}, bf16[128,192]{0,1:T(8,128)(2,1)}, u32[]{:S(2)}) copy-start(bf16[128,192]{0,1:T(8,128)(2,1)} %param.14) | copy-start | bytes 147460
  117.7 162.0 %reduce-scatter.5.cloned.1.call-start = ((), (), s32[]{:S(2)}) async-start(), calls=%async_computation.4 | async-start | bytes 147456 | tf_op jit(solution)/shard_map/reduce_scatter | solution.py:103
  257.8 10.2 %copy-start = (f32[384,2304]{0,1:T(8,128)S(1)}, f32[384,2304]{0,1:T(8,128)}, u32[]{:S(2)}) copy-start(f32[384,2304]{0,1:T(8,128)} %all-reduce.3.cloned.1.call-done) | copy-start | bytes 10616836
  268.0 2.1 copy-start.3
  270.0 1.3 copy-start.1
  270.1 1.0 copy-start.4
  271.8 1.2 copy-start.2
  272.9 18.2 %reduce-scatter.3.cloned.1.call-start = ((), (), s32[]{:S(2)}) async-start(), calls=%async_computation.3 | async-start | bytes 147456 | tf_op jit(solution)/shard_map/reduce_scatter | solution.py:100
Sparse Core Ops, SparseCore 0:
  117.8 140.0 all-reduce.2
  273.1 6.5 reduce-scatter.4
  282.5 8.6 reduce-scatter.2
where the time goes:
time: 298 us
  waiting for transfers between devices  150 us (50%)
  blocking collectives  110 us (37%)
  between operations  13.9 us (5%)
  matrix products  10.6 us (4%)
  other arithmetic  9.59 us (3%)
  local copies, waits for them, and re-layouts  3.61 us (1%)
    psum x1, waiting for transfers between devices, shards(): lax.psum(jnp.concatenate([contract_rows(keys, d_gate), contract_rows(keys...  133 us
    all_gather x1, blocking collectives, shards(): lax.all_gather(gate_weight, 'tok', axis=0, tiled=True)  33.4 us
    all_gather x1, blocking collectives, shards(): lax.all_gather(down_weight, 'tok', axis=0, tiled=True)  31.4 us
    all_gather x1, blocking collectives, shards(): lax.all_gather(up_weight, 'tok', axis=0, tiled=True)  31.3 us
    reduce_scatter x1, waiting for transfers between devices, shards(): lax.psum_scatter(out_part.astype(jnp.bfloat16), 'hid', scatter_dimension=...  11.5 us
  transfers between devices with their start and end apart: 3, of which 3 were waited for; matrix products, arithmetic and copies ran while one was open for 1% of the time, Pallas kernels for 0%

commit v1 on v0

--- a/solution.py
+++ b/solution.py
@@ -50,16 +50,19 @@
     d_gate = (-back * key_up * silu_slope(key_gate)).astype(jnp.bfloat16)
     d_up = (-back * gate_act).astype(jnp.bfloat16)
     width = gate_weight.shape[1]
-    grads = lax.psum(
-        jnp.concatenate(
-            [
-                contract_rows(keys, d_gate),
-                contract_rows(keys, d_up),
-                -contract_rows(scaled, key_act),
-            ],
-            axis=1,
+    grads = jnp.sum(
+        lax.all_gather(
+            jnp.concatenate(
+                [
+                    contract_rows(keys, d_gate),
+                    contract_rows(keys, d_up),
+                    -contract_rows(scaled, key_act),
+                ],
+                axis=1,
+            ),
+            "tok",
         ),
-        "tok",
+        axis=0,
     )
     olds = (w_gate, w_up, w_down)
     pieces = [grads[:, :width], grads[:, width : 2 * width], grads[:, 2 * width :]]

time: 298 us -> 749 us (2.51)
  waiting for transfers between devices: 150 us -> 551 us
  other arithmetic: 9.59 us -> 43.5 us
  local copies, waits for them, and re-layouts: 3.61 us -> 18.4 us
    all_gather x0 -> x1, waiting for transfers between devices: none -> 533 us  [shards(): lax.all_gather(jnp.concatenate([contract_rows(keys, d_gate), contract_row...]
    psum x1 -> x0, waiting for transfers between devices: 133 us -> none  [shards(): lax.psum(jnp.concatenate([contract_rows(keys, d_gate), contract_rows(keys...]
    reduce_sum x0 -> x1, other arithmetic: none -> 36.4 us  [shards(): jnp.sum(lax.all_gather(jnp.concatenate([contract_rows(keys, d_gate), cont...]
    unnamed x22 -> x25, local copies, waits for them, and re-layouts: 0.38 us -> 15.2 us
where the time goes in v1:
time: 749 us; the launch traced here: 748 us
  waiting for transfers between devices  551 us (74%)
  blocking collectives  111 us (15%)
  other arithmetic  43.5 us (6%)
  local copies, waits for them, and re-layouts  18.4 us (2%)
  between operations  14 us (2%)
  matrix products  10.5 us (1%)
    all_gather x1, waiting for transfers between devices, shards(): lax.all_gather(jnp.concatenate([contract_rows(keys, d_gate), contract_row...  533 us
    reduce_sum x1, other arithmetic, shards(): jnp.sum(lax.all_gather(jnp.concatenate([contract_rows(keys, d_gate), cont...  36.4 us
    all_gather x1, blocking collectives, shards(): lax.all_gather(gate_weight, 'tok', axis=0, tiled=True)  33.4 us
    all_gather x1, blocking collectives, shards(): lax.all_gather(down_weight, 'tok', axis=0, tiled=True)  31.7 us
    all_gather x1, blocking collectives, shards(): lax.all_gather(up_weight, 'tok', axis=0, tiled=True)  31.5 us
    unnamed x25, local copies, waits for them, and re-layouts  15.2 us
  transfers between devices with their start and end apart: 3, of which 3 were waited for; matrix products, arithmetic and copies ran while one was open for 1% of the time, Pallas kernels for 0%

profile of v1, /device:TPU:0, one launch (start us, length us, event | category | flops | bytes accessed | tf_op | source)
XLA Modules:
  0.0 748.2 jit_solution(9852515682568368971)
XLA Ops:
  7.2 2.7 all_gather.30
  9.9 33.4 %all_gather.27 = bf16[384,768]{1,0:T(8,128)(2,1)S(1)} all-gather(bf16[48,768]{1,0:T(8,128)(2,1)} %param.11), channel_id=1, replica_groups=mesh['scene'=2,'tok'=8,'hid'=2] {'tok'}, dimensions={0}, use_global_device_ids=true | all-gather | bytes 663552 | tf_op jit(solution)/shard_map/all_gather | solution.py:40
  43.3 31.5 %all_gather.31 = bf16[384,768]{1,0:T(8,128)(2,1)S(1)} all-gather(bf16[48,768]{1,0:T(8,128)(2,1)} %param.12), channel_id=1, replica_groups=mesh['scene'=2,'tok'=8,'hid'=2] {'tok'}, dimensions={0}, use_global_device_ids=true | all-gather | bytes 663552 | tf_op jit(solution)/shard_map/all_gather | solution.py:41
  74.8 1.0 fusion.34
  75.9 1.0 fusion.33
  76.9 2.4 all_gather.28
  79.3 31.7 %all_gather.29 = bf16[384,768]{1,0:T(8,128)(2,1)S(1)} all-gather(bf16[48,768]{1,0:T(8,128)(2,1)S(1)} %copy-done.8), channel_id=1, replica_groups=mesh['scene'=2,'tok'=8,'hid'=2] {'tok'}, dimensions={0}, use_global_device_ids=true | all-gather | bytes 663552 | tf_op jit(solution)/shard_map/all_gather | solution.py:42
  111.1 1.0 fusion.20
  112.1 1.2 fusion.6
  113.3 1.5 fusion.4
  114.8 1.3 fusion.5
  116.1 2.1 pad_maximum_fusion
  118.3 1.1 copy.15
  119.3 1.1 copy.17
  120.4 1.1 copy.18
  121.5 2.0 all_gather.35
  123.5 2.2 all_gather.34
  125.6 533.0 %all-gather.3.cloned.1.call-done = f32[3072,2304]{0,1:T(8,128)} async-done(((f32[384,2304]{0,1:T(8,128)}), f32[3072,2304]{0,1:T(8,128)}) %all-gather.3.cloned.1.call-update) | async-done | bytes 28311568 | tf_op jit(solution)/shard_map/all_gather | solution.py:54
  658.7 15.0 %copy.20 = f32[288,8,8,384]{3,2,1,0:T(8,128)S(1)} copy(f32[288,8,8,384]{3,1,2,0:T(8,128)} %bitcast.31) | data formatting | bytes 56623104
  673.7 36.4 %bitcast_reduce_fusion = f32[384,2304]{0,1:T(8,128)S(1)} fusion(f32[288,8,8,384]{3,2,1,0:T(8,128)S(1)} %copy.20), kind=kLoop, calls=%fused_computation | loop fusion | flops 6193152 | bytes 31850496 | tf_op jit(solution)/shard_map/reduce_sum | solution.py:53
  710.2 1.5 multiply_reduce_fusion.2
  711.6 4.6 all-reduce
  716.2 0.7 rsqrt_multiply_fusion.5
  716.9 0.8 rsqrt_multiply_fusion.1
  717.7 2.0 fusion.9
  719.8 0.3 convolution_bitcast_fusion.1
  720.1 0.3 convolution_bitcast_fusion.2
  720.9 0.5 fusion.24
  721.4 1.1 fusion.19
  722.5 1.0 convolution_convert_fusion
  723.6 6.6 reduce-scatter.5.cloned.1.call-done
  730.1 11.5 %reduce-scatter.3.cloned.1.call-done = bf16[128,192]{0,1:T(8,128)(2,1)} async-done(((bf16[128,384]{0,1:T(8,128)(2,1)}), bf16[128,192]{0,1:T(8,128)(2,1)}) %reduce-scatter.3.cloned.1.call-update) | async-done | bytes 49168 | tf_op jit(solution)/shard_map/reduce_scatter | solution.py:103
  (31 shorter events, 0.7 us)
Async XLA Ops:
  7.2 651.5 %all-gather.3.cloned.1.call-start = ((), (), s32[]{:S(2)}) async-start(), calls=%async_computation.4 | async-start | bytes 31850496 | tf_op jit(solution)/shard_map/all_gather | solution.py:54
  75.9 1.1 copy-start.7
  75.9 3.4 copy-start.8
  75.9 35.2 %copy-start.11 = (f32[1024]{0:T(1024)S(1)}, f32[1024]{0:T(1024)}, u32[]{:S(2)}) copy-start(f32[1024]{0:T(1024)} %param.10) | copy-start | bytes 12292
  118.2 3.2 copy-start.9
  118.2 5.2 copy-start.10
  118.2 611.9 %reduce-scatter.5.cloned.1.call-start = ((), (), s32[]{:S(2)}) async-start(), calls=%async_computation.3 | async-start | bytes 147456 | tf_op jit(solution)/shard_map/reduce_scatter | solution.py:106
  673.7 36.4 %copy-start = (bf16[384,768]{0,1:T(8,128)(2,1)S(1)}, bf16[384,768]{0,1:T(8,128)(2,1)}, u32[]{:S(2)}) copy-start(bf16[384,768]{0,1:T(8,128)(2,1)} %copy.15) | copy-start | bytes 1769476
  673.7 36.4 %copy-start.1 = (bf16[384,768]{0,1:T(8,128)(2,1)S(1)}, bf16[384,768]{0,1:T(8,128)(2,1)}, u32[]{:S(2)}) copy-start(bf16[384,768]{0,1:T(8,128)(2,1)} %copy.17) | copy-start | bytes 1769476
  673.7 36.4 %copy-start.2 = (bf16[384,768]{0,1:T(8,128)(2,1)S(1)}, bf16[384,768]{0,1:T(8,128)(2,1)}, u32[]{:S(2)}) copy-start(bf16[384,768]{0,1:T(8,128)(2,1)} %copy.18) | copy-start | bytes 1769476
  717.7 2.1 copy-start.5
  717.7 2.9 copy-start.6
  719.8 0.8 copy-start.3
  720.9 1.6 copy-start.4
  722.4 19.2 %reduce-scatter.3.cloned.1.call-start = ((), (), s32[]{:S(2)}) async-start(), calls=%async_computation.2 | async-start | bytes 147456 | tf_op jit(solution)/shard_map/reduce_scatter | solution.py:103
Sparse Core Ops, SparseCore 0:
  118.4 540.2 all-gather.2
  722.6 7.5 reduce-scatter.4
  732.9 8.6 reduce-scatter.2
